TPU v7x, 256 devices: a whole 4x4x8 slice. The times are simulated.
256 devices in a mesh: param: 16 (over z, core), ex: 16 (over x, y).
Axes of the slice: x: 4, y: 4, z: 8, core: 2. Of those that a mesh axis runs over, the one named last changes fastest.
Arguments:
- query_acts: bfloat16 [16, 256, 16, 4096], P(None, 'ex', None, 'param'), may hold values from -6 to 6
- query_grads: bfloat16 [16, 256, 16, 4096], P(None, 'ex', None, 'param'), may hold values from -6 to 6
- train_acts: bfloat16 [16, 512, 16, 4096], P(None, 'ex', None, 'param'), as said below
- train_grads: bfloat16 [16, 512, 16, 4096], P(None, 'ex', None, 'param'), as said below
- input_projection: bfloat16 [4096, 128], P('param'), as said below
- proj_out: bfloat16 [4096, 64], P('param'), as said below
- query_clusters: int32 [16, 256], P('param'), may hold values from 0 to 127
- train_clusters: int32 [16, 512], P(None, 'ex'), may hold values from 0 to 127
- pair_mask: int32 [128, 128], replicated, may hold values 0 or 1
Outputs:
- scores: float32 [16, 256, 16, 512], P('param', None, None, 'ex')
- cluster_scores: float32 [16, 256, 128], P('param', 'ex')
Inputs may be any that keep to these rules, and one draw needn't show every extreme that they name: `train_acts`: token features whose scales differ from token to token and from example to example. `train_grads`: token gradients whose scales differ from example to example. `input_projection`: random projection columns of differing scales. `proj_out`: random projection columns of differing scales.
All inputs are finite; a program needn't handle non-finite values.
Results may differ from a plain program's by a relative error of at most 0.022.
The roundings to bfloat16 on the way count: a program that leaves them out, or rounds other values in their place, can miss the bound.
Values may be sent and summed in bfloat16 or wider, within the bound.
A program may use at most 128 MiB of HBM per device.

v0:
```python
import math

import jax
import jax.numpy as jnp
from jax import lax
from jax.sharding import PartitionSpec as P


def inverse_of(gram, count):
    mean = gram / count
    size = gram.shape[0]
    damping = 0.1 * jnp.trace(mean) / size
    identity = jnp.eye(size, dtype=gram.dtype)
    factor = jnp.linalg.cholesky(mean + damping * identity)
    return jax.scipy.linalg.cho_solve((factor, True), identity)


def form_grads(part_out, part_in):
    examples = part_out.shape[0]
    grad = jnp.einsum("tkr,tks->trs", part_out, part_in, preferred_element_type=jnp.float32)
    return grad.reshape(examples, -1).astype(jnp.bfloat16)


def shards(
    query_acts,
    query_grads,
    train_acts,
    train_grads,
    input_projection,
    proj_out,
    query_clusters,
    train_clusters,
    pair_mask,
):
    group_batches = train_acts.shape[0]
    query_rows = query_acts.shape[1]
    train_rows = train_acts.shape[1]
    tokens = train_acts.shape[2]
    width_in = input_projection.shape[1]
    width_out = proj_out.shape[1]
    clusters = pair_mask.shape[0]
    pieces = []
    for acts, grads in ((query_acts, query_grads), (train_acts, train_grads)):
        lead = acts.shape[:3]
        flat_acts = acts.reshape(-1, acts.shape[3])
        flat_grads = grads.reshape(-1, grads.shape[3])
        joined = jnp.concatenate(
            [
                jnp.dot(flat_acts, input_projection, preferred_element_type=jnp.float32),
                jnp.dot(flat_grads, proj_out, preferred_element_type=jnp.float32),
            ],
            axis=1,
        )
        pieces.append(joined.reshape(lead + (width_in + width_out,)))
    projected = lax.psum_scatter(
        jnp.concatenate(pieces, axis=1), "param", scatter_dimension=0, tiled=True
    ).astype(jnp.bfloat16)
    factors = projected[0]
    query_in = factors[:query_rows, :, :width_in]
    query_output_side = factors[:query_rows, :, width_in:]
    train_in = factors[query_rows:, :, :width_in]
    train_out = factors[query_rows:, :, width_in:]
    flat_in = train_in.reshape(-1, width_in)
    flat_out = train_out.reshape(-1, width_out)
    gram_in = jnp.dot(flat_in.T, flat_in, preferred_element_type=jnp.float32)
    gram_out = jnp.dot(flat_out.T, flat_out, preferred_element_type=jnp.float32)
    gram_in, gram_out = lax.psum((gram_in, gram_out), ("param", "ex"))
    total_train = group_batches * train_rows * lax.axis_size("ex")
    count = float(total_train * tokens)
    inv_in = inverse_of(gram_in, count)
    inv_out = inverse_of(gram_out, count)
    preconditioned_input = jnp.dot(
        query_in.reshape(-1, width_in).astype(jnp.float32), inv_in, precision=lax.Precision.HIGHEST
    ).reshape(query_rows, tokens, width_in)
    preconditioned_output = jnp.dot(
        query_output_side.reshape(-1, width_out).astype(jnp.float32),
        inv_out,
        precision=lax.Precision.HIGHEST,
    ).reshape(query_rows, tokens, width_out)
    query_before_preconditioning = jnp.einsum(
        "bui,bux->bix", preconditioned_output, preconditioned_input, precision=lax.Precision.HIGHEST
    )
    query_before_preconditioning = query_before_preconditioning.reshape(query_rows, -1).astype(
        jnp.bfloat16
    )
    trains = lax.all_gather(form_grads(train_out, train_in), "param", axis=0, tiled=True)
    cluster_ids = jnp.arange(clusters, dtype=jnp.int32)
    train_onehot = train_clusters.reshape(-1)[:, None] == cluster_ids[None, :]
    train_side = train_onehot.astype(jnp.bfloat16)
    mask_values = pair_mask.astype(jnp.bfloat16)
    scale = 1.0 / (tokens * math.sqrt(width_in * width_out))
    contract = (((1,), (1,)), ((), ()))
    ids = query_clusters[0]
    query_onehot = (ids[:, None] == cluster_ids[None, :]).astype(jnp.bfloat16)
    picked = jnp.dot(query_onehot, mask_values, preferred_element_type=jnp.float32).astype(
        jnp.bfloat16
    )
    allowed = lax.dot_general(picked, train_side, contract, preferred_element_type=jnp.float32)
    raw = lax.dot_general(
        lax.all_gather(query_before_preconditioning, "ex", axis=0, tiled=True),
        trains,
        contract,
        preferred_element_type=jnp.float32,
    )
    scores = raw * scale * allowed
    partial_value = jnp.dot(
        scores, train_onehot.astype(jnp.float32), precision=lax.Precision.HIGHEST
    ) * math.sqrt(clusters / total_train)
    summed = lax.psum_scatter(
        partial_value.astype(jnp.bfloat16), "ex", scatter_dimension=0, tiled=True
    ).astype(jnp.float32)
    all_queries = scores.shape[0]
    return (
        scores.reshape(1, all_queries, group_batches, train_rows),
        summed.reshape(1, summed.shape[0], clusters),
    )


def solution(mesh):
    return jax.shard_map(
        shards,
        mesh=mesh,
        in_specs=(
            P(None, "ex", None, "param"),
            P(None, "ex", None, "param"),
            P(None, "ex", None, "param"),
            P(None, "ex", None, "param"),
            P("param", None),
            P("param", None),
            P("param", None),
            P(None, "ex"),
            P(),
        ),
        out_specs=(P("param", None, None, "ex"), P("param", "ex", None)),
        check_vma=False,
    )
```

profile of v0, /device:TPU:2, one launch (start us, length us, event | category | flops | bytes accessed | tf_op | source)
XLA Modules:
  0.0 642.3 jit_solution(12987489176357474776)
XLA Ops:
  7.2 3.8 fusion.27
  11.1 1.4 fusion.28
  12.5 3.1 pad_maximum_fusion.1
  15.6 8.4 %copy.28 = f32[8192,192]{1,0:T(8,128)} copy(f32[8192,192]{0,1:T(8,128)} %pad_maximum_fusion.1) | data formatting | bytes 12582912 | tf_op jit(solution)/shard_map/concatenate | solution.py:47
  24.1 13.1 %copy.30 = f32[16,32,16,192]{3,1,2,0:T(8,128)} copy(f32[16,32,16,192]{3,2,1,0:T(8,128)} %bitcast.70) | data formatting | bytes 12582912 | tf_op jit(solution)/shard_map/reshape | solution.py:54
  37.2 0.8 fusion.25
  39.5 2.0 pad_maximum_fusion.2
  41.4 5.1 copy.27
  46.6 7.4 %copy.29 = f32[16,16,16,192]{3,1,2,0:T(8,128)} copy(f32[16,16,16,192]{3,2,1,0:T(8,128)} %bitcast.71) | data formatting | bytes 6291456 | tf_op jit(solution)/shard_map/reshape | solution.py:54
  54.0 11.0 %pad_maximum_fusion = f32[16,48,16,192]{3,1,2,0:T(8,128)} fusion(f32[16,32,16,192]{3,1,2,0:T(8,128)} %copy.30, f32[16,16,16,192]{3,1,2,0:T(8,128)} %copy.29), kind=kLoop, calls=%fused_computation | loop fusion | flops 2359296 | bytes 18874368 | tf_op jit(solution)/shard_map/concatenate | solution.py:56
  65.1 82.4 %reduce-scatter.2.cloned.1.call-done = f32[1,48,16,192]{3,1,2,0:T(8,128)} async-done(((f32[16,48,16,192]{3,1,2,0:T(8,128)}), f32[1,48,16,192]{3,1,2,0:T(8,128)}) %reduce-scatter.2.cloned.1.call-update) | async-done | bytes 589840 | tf_op jit(solution)/shard_map/reduce_scatter | solution.py:55
  147.4 1.2 convert_bitcast_fusion
  148.6 0.9 convolution_bitcast_fusion.1
  149.8 75.2 %psum.14 = f32[64,64]{1,0:T(8,128)S(1)} all-reduce(f32[64,64]{1,0:T(8,128)S(1)} %convolution_bitcast_fusion.3), channel_id=1, replica_groups=mesh['param'=16,'ex'=16] {'param','ex'}, use_global_device_ids=true, to_apply=%region_1.0 | all-reduce | flops 4096 | bytes 32768 | tf_op jit(solution)/shard_map/psum | solution.py:67
  226.4 5.8 cholesky.33
  233.6 4.9 custom-call.20
  239.1 155.0 %all-reduce.4.cloned.1.call-done = f32[128,128]{1,0:T(8,128)} async-done(((f32[128,128]{1,0:T(8,128)}), f32[128,128]{1,0:T(8,128)}) %all-reduce.4.cloned.1.call-update) | async-done | bytes 65552 | tf_op jit(solution)/shard_map/psum | solution.py:67
  394.1 1.5 select_reduce_fusion.1
  396.3 0.9 select_add_fusion
  397.2 0.9 fusion.9
  398.1 11.7 %cholesky.68 = f32[128,128]{1,0:T(8,128)S(1)} custom-call(f32[128,128]{1,0:T(8,128)S(1)} %fusion.9), custom_call_target="Cholesky" | custom-call | tf_op jit(solution)/shard_map/jit(cholesky)/cholesky | solution.py:14
  411.1 9.8 %custom-call.21 = f32[1,128,128]{1,2,0:T(8,128)S(1)} custom-call(f32[1,128,128]{2,1,0:T(8,128)S(1)} %fusion.5), custom_call_target="InvertDiagBlocksLowerTriangular" | custom-call | tf_op jit(solution)/shard_map/jit(_cho_solve)/triangular_solve | solution.py:15
  421.6 1.0 convolution_convert_fusion.1
  422.6 0.9 copy.51
  424.0 1.1 copy.50
  425.5 51.9 %all-gather.3.cloned.1.call-done = bf16[256,8192]{1,0:T(8,128)(2,1)} async-done(((bf16[16,8192]{1,0:T(8,128)(2,1)}), bf16[256,8192]{1,0:T(8,128)(2,1)}) %all-gather.3.cloned.1.call-update) | async-done | bytes 4194320 | tf_op jit(solution)/shard_map/all_gather | solution.py:100
  477.5 57.9 %all-gather.5.cloned.1.call-done = bf16[512,8192]{1,0:T(8,128)(2,1)} async-done(((bf16[32,8192]{1,0:T(8,128)(2,1)}), bf16[512,8192]{1,0:T(8,128)(2,1)}) %all-gather.5.cloned.1.call-update) | async-done | bytes 8388624 | tf_op jit(solution)/shard_map/all_gather | solution.py:86
  535.3 7.2 %convolution_multiply_fusion.1 = f32[256,512]{1,0:T(8,128)S(1)} fusion(bf16[256,8192]{1,0:T(8,128)(2,1)} %all-gather.3.cloned.1.call-done, bf16[512,8192]{1,0:T(8,128)(2,1)} %all-gather.5.cloned.1.call-done), kind=kOutput, calls=%fused_computation.5 | convolution fusion | flops 2147614720 | bytes 13107200 | tf_op jit(solution)/shard_map/dot_general | solution.py:99
  542.9 1.1 fusion
  545.3 1.0 copy.37
  546.3 88.2 %all-reduce.6.cloned.1.call-done = bf16[256,128]{1,0:T(8,128)(2,1)} async-done(((bf16[256,128]{1,0:T(8,128)(2,1)}), bf16[256,128]{1,0:T(8,128)(2,1)}) %all-reduce.6.cloned.1.call-update) | async-done | bytes 65552
  634.5 1.3 bitcast_convert_fusion
  (57 shorter events, 8.4 us)
Async XLA Ops:
  7.2 30.0 %copy-start = (bf16[16,16,16,256]{3,2,1,0:T(8,128)(2,1)S(1)}, bf16[16,16,16,256]{3,2,1,0:T(8,128)(2,1)}, u32[]{:S(2)}) copy-start(bf16[16,16,16,256]{3,2,1,0:T(8,128)(2,1)} %param.9) | copy-start | bytes 6291460
  7.2 140.3 %reduce-scatter.2.cloned.1.call-start = ((), (), s32[]{:S(2)}) async-start(), calls=%async_computation.1 | async-start | bytes 13369344 | tf_op jit(solution)/shard_map/reduce_scatter | solution.py:55
  7.2 3.9 copy-start.2
  7.2 3.9 copy-start.5
  24.1 13.1 %copy-start.4 = (bf16[256,128]{1,0:T(8,128)(2,1)S(1)}, bf16[256,128]{1,0:T(8,128)(2,1)}, u32[]{:S(2)}) copy-start(bf16[256,128]{1,0:T(8,128)(2,1)} %param.13) | copy-start | bytes 196612
  37.1 1.6 copy-start.3
  65.0 360.5 %copy-start.7 = (s32[16,32]{1,0:T(8,128)S(1)}, s32[16,32]{1,0:T(8,128)}, u32[]{:S(2)}) copy-start(s32[16,32]{1,0:T(8,128)} %param.16) | copy-start | bytes 6148
  65.0 329.1 %all-reduce.4.cloned.1.call-start = ((), (), s32[]{:S(2)}) async-start(), calls=%async_computation.2 | async-start | bytes 131072 | tf_op jit(solution)/shard_map/psum | solution.py:67
  149.7 327.7 %all-gather.3.cloned.1.call-start = ((), (), s32[]{:S(2)}) async-start(), calls=%async_computation.3 | async-start | bytes 4456448 | tf_op jit(solution)/shard_map/all_gather | solution.py:100
  423.6 111.8 %all-gather.5.cloned.1.call-start = ((), (), s32[]{:S(2)}) async-start(), calls=%async_computation.4 | async-start | bytes 8912896 | tf_op jit(solution)/shard_map/all_gather | solution.py:86
  425.2 209.3 %all-reduce.6.cloned.1.call-start = ((), (), s32[]{:S(2)}) async-start(), calls=%async_computation.5 | async-start | bytes 131072
  425.5 117.0 %copy-start.6 = (s32[128,128]{1,0:T(8,128)S(1)}, s32[128,128]{1,0:T(8,128)}, u32[]{:S(2)}) copy-start(s32[128,128]{1,0:T(8,128)} %param.17) | copy-start | bytes 196612
  425.5 117.0 %copy-start.8 = (s32[1,256]{1,0:T(1,128)S(1)}, s32[1,256]{1,0:T(1,128)}, u32[]{:S(2)}) copy-start(s32[1,256]{1,0:T(1,128)} %param.15) | copy-start | bytes 3076
  425.5 118.5 %copy-start.9 = (u32[256]{0:T(256)S(1)}, u32[256]{0:T(256)}, u32[]{:S(2)}) copy-start(u32[256]{0:T(256)} %constant.124) | copy-start | bytes 3076
  535.3 100.4 %copy-start.1 = (bf16[16,16,16,256]{3,2,1,0:T(8,128)(2,1)S(1)}, bf16[16,16,16,256]{3,2,1,0:T(8,128)(2,1)}, u32[]{:S(2)}) copy-start(bf16[16,16,16,256]{3,2,1,0:T(8,128)(2,1)} %param.9) | copy-start | bytes 6291460
Sparse Core Ops, SparseCore 0:
  65.1 82.2 reduce-scatter.1
  153.5 240.5 all-reduce.3
  423.7 53.7 all-gather.2
  479.7 55.5 all-gather.4
  544.2 90.2 all-reduce.5
where the time goes:
time: 643 us; the launch traced here: 642 us
  waiting for transfers between devices  436 us (68%)
  blocking collectives  75.2 us (12%)
  other arithmetic  57.3 us (9%)
  local copies, waits for them, and re-layouts  38.8 us (6%)
  matrix products  19.1 us (3%)
  between operations  16 us (2%)
    psum x1, waiting for transfers between devices, shards(): gram_in, gram_out = lax.psum((gram_in, gram_out), ('param', 'ex'))  155 us
    unnamed x6, waiting for transfers between devices  88.3 us
    reduce_scatter x1, waiting for transfers between devices, shards(): lax.psum_scatter(jnp.concatenate(pieces, axis=1), 'param', scatter_dimens...  82.4 us
    psum x1, blocking collectives, shards(): gram_in, gram_out = lax.psum((gram_in, gram_out), ('param', 'ex'))  75.2 us
    all_gather x1, waiting for transfers between devices, shards(): lax.all_gather(form_grads(train_out, train_in), 'param', axis=0, tiled=True)  57.9 us
    all_gather x1, waiting for transfers between devices, shards(): lax.all_gather(query_before_preconditioning, 'ex', axis=0, tiled=True)  51.9 us
    reshape x2, local copies, waits for them, and re-layouts, shards(): pieces.append(joined.reshape(lead + (width_in + width_out,)))  20.5 us
    another operation x6, other arithmetic, inverse_of(): factor = jnp.linalg.cholesky(mean + damping * identity)  18.9 us
  transfers between devices with their start and end apart: 5, of which 5 were waited for; matrix products, arithmetic and copies ran while one was open for 3% of the time, Pallas kernels for 0%

commit v1 on v0

v1 whole, which is shorter than its diff:
```python
import functools
import math

import jax
import jax.numpy as jnp
from jax import lax
from jax.experimental import pallas as pl
from jax.experimental.pallas import tpu as pltpu
from jax.sharding import PartitionSpec as P

MESH = pl.DeviceIdType.MESH
F32 = jnp.float32
BF16 = jnp.bfloat16
NT = (((1,), (1,)), ((), ()))
TN = (((0,), (0,)), ((), ()))

T_IN, T_ALL = 512, 768
Q_IN, ALL = 256, 1152
Q_ALL = ALL - T_ALL


def remote(src, dst, send, recv, device):
    return pltpu.make_async_remote_copy(
        src_ref=src, dst_ref=dst, send_sem=send, recv_sem=recv, device_id=device, device_id_type=MESH
    )


def spot(p, e):
    return {"param": p, "ex": e}


def halves(chunk):
    size = (T_ALL, Q_ALL)[chunk] // 2
    return (pl.ds(0, size), pl.ds(size, size))


def reduce_kernel(
    nz,
    qa, qg, ta, tg, win, wout,
    out,
    qa_b, qg_b, ta_b, tg_b, part_t, part_q, sib_t, sib_q, snd_t, snd_q, rcv_t, rcv_q,
    in_sem, sib_send, sib_recv, ring_send, ring_recv,
):
    p, e = lax.axis_index("param"), lax.axis_index("ex")
    z, c = p // 2, p % 2
    sibling = spot(z * 2 + 1 - c, e)
    ring = (spot(lax.rem(z + 1, nz) * 2 + c, e), spot(lax.rem(z + nz - 1, nz) * 2 + c, e))
    far = nz // 2

    def shift(k):
        m = far - (k + 1) // 2
        return jnp.where(k % 2 == 1, m, nz - m) % nz

    def group(u):
        k = u // 2
        core = jnp.where(u % 2 == 0, 1 - c, c)
        return lax.rem(z + shift(k), nz) * 2 + core

    pairs = ((ta, ta_b), (tg, tg_b), (qa, qa_b), (qg, qg_b))

    def loads(u):
        g = group(u)
        return [
            pltpu.make_async_copy(src.at[g], dst.at[u], in_sem.at[i, u])
            for i, (src, dst) in enumerate(pairs)
        ]

    def start(u, carry):
        for copy in loads(u):
            copy.start()
        return carry

    lax.fori_loop(0, 2 * nz, start, 0)
    barrier = pltpu.get_barrier_semaphore()
    for device in (sibling,) + ring:
        pl.semaphore_signal(barrier, inc=1, device_id=device, device_id_type=MESH)
    pl.semaphore_wait(barrier, 3)

    w_in = win[...]
    narrow = wout[...].astype(F32).T
    blank = jnp.zeros_like(narrow)
    w_low = jnp.concatenate([narrow, blank], axis=1).astype(BF16)
    w_high = jnp.concatenate([blank, narrow], axis=1).astype(BF16)

    def dot(a, b):
        return jnp.dot(a, b, preferred_element_type=F32)

    parts, sibs, sends, recvs = (part_t, part_q), (sib_t, sib_q), (snd_t, snd_q), (rcv_t, rcv_q)

    def to_sibling(k, chunk):
        return remote(
            parts[chunk].at[0, k], sibs[chunk].at[k], sib_send.at[chunk, k], sib_recv.at[chunk, k], sibling
        )

    def project(u, carry):
        for copy in loads(u):
            copy.wait()
        k, own = u // 2, u % 2
        part_t[own, k, 0:T_IN, :] = dot(ta_b[u], w_in).astype(BF16)
        part_t[own, k, T_IN:T_ALL, :] = (
            dot(tg_b[u, 0:256, :], w_low) + dot(tg_b[u, 256:512, :], w_high)
        ).astype(BF16)

        @pl.when(own == 0)
        def _():
            to_sibling(k, 0).start()

        part_q[own, k, 0:Q_IN, :] = dot(qa_b[u], w_in)
        part_q[own, k, Q_IN:Q_ALL, :] = dot(qg_b[u, 0:128, :], w_low) + dot(qg_b[u, 128:256, :], w_high)

        @pl.when(own == 0)
        def _():
            to_sibling(k, 1).start()

        return carry

    def hop(way, step, chunk, half):
        rows = halves(chunk)[half]
        return remote(
            sends[chunk].at[way, step, rows],
            recvs[chunk].at[way, step, rows],
            ring_send.at[way, step, chunk, half],
            ring_recv.at[way, step, chunk, half],
            ring[way],
        )

    def own_sum(k, chunk, rows):
        return parts[chunk][1, k, rows, :].astype(F32) + sibs[chunk][k, rows, :].astype(F32)

    hops = []

    def send(way, step, chunk, half):
        rows = halves(chunk)[half]
        k = 0 if step == 0 else 2 * step - 1 + way
        value = own_sum(k, chunk, rows)
        if step >= 2 or (step == 1 and half == way):
            hop(way, step - 1, chunk, half).wait_recv()
            value = value + recvs[chunk][way, step - 1, rows, :].astype(F32)
        sends[chunk][way, step, rows, :] = value.astype(sends[chunk].dtype)
        copy = hop(way, step, chunk, half)
        copy.start()
        hops.append(copy)

    def round_of(step, chunk):
        if step == 0:
            for way in (0, 1):
                send(way, 0, chunk, way)
            return
        for late in (1, 0):
            for way in (0, 1):
                send(way, step, chunk, way if late == 0 else 1 - way)

    for step in range(far):
        low, high = (0, 2) if step == 0 else (4 * step - 2, 4 * step + 2)
        lax.fori_loop(low, high, project, 0)
        for k in range(low // 2, high // 2):
            to_sibling(k, 0).wait_recv()
            to_sibling(k, 1).wait_recv()
        round_of(step, 0)
    round_of(0, 1)
    lax.fori_loop(2 * nz - 2, 2 * nz, project, 0)
    to_sibling(nz - 1, 0).wait_recv()
    to_sibling(nz - 1, 1).wait_recv()

    def final(chunk):
        for half in (1, 0):
            rows = halves(chunk)[half]
            value = own_sum(nz - 1, chunk, rows)
            for way in (0, 1):
                hop(way, far - 1, chunk, half).wait_recv()
                value = value + recvs[chunk][way, far - 1, rows, :].astype(F32)
            out[pl.ds(T_ALL * chunk + rows.start, rows.size), :] = value.astype(BF16)

    for step in range(1, far):
        round_of(step, 1)
    final(0)
    final(1)
    for copy in hops:
        copy.wait_send()
    for k in range(nz):
        to_sibling(k, 0).wait_send()
        to_sibling(k, 1).wait_send()


def newton(damped, level, steps, scalings):
    size = damped.shape[0]
    rows = lax.broadcasted_iota(jnp.int32, (size, size), 0)
    eye = (rows == lax.broadcasted_iota(jnp.int32, (size, size), 1)).astype(F32)

    def dot(a, b):
        return jnp.dot(a, b, preferred_element_type=F32, precision=lax.Precision.HIGHEST)

    resid = eye - level * damped
    guess = level * eye
    for index in range(steps):
        c = scalings[index]
        grown = guess + (level * resid if index == 0 else dot(guess, resid))
        resid = (1.0 - c) * eye + c * dot(resid, resid)
        guess = c * grown
    for _ in range(2):
        resid = eye - dot(damped, guess)
        guess = guess + dot(guess, resid)
    return 0.5 * (guess + guess.T)


def schedule_of(size):
    kappa = 1.0 + 10.0 * size
    rho = (kappa - 1.0) / (kappa + 1.0)
    scalings = []
    while rho > 1e-4:
        scalings.append(2.0 / (2.0 - rho * rho))
        rho = rho * rho / (2.0 - rho * rho)
    return 2.0 / (1.0 + kappa), scalings


def inverse_of(gram, count):
    size = gram.shape[0]
    mean = gram * (1.0 / count)
    rows = lax.broadcasted_iota(jnp.int32, (size, size), 0)
    diagonal = rows == lax.broadcasted_iota(jnp.int32, (size, size), 1)
    floor = 0.1 / size * jnp.sum(jnp.where(diagonal, mean, 0.0), keepdims=True)
    damped = mean + jnp.where(diagonal, floor, 0.0)
    level, scalings = schedule_of(size)
    return newton(damped, level / floor, len(scalings), scalings)


def score_kernel(
    nz, ne, count, scale, spread,
    fac, query_ids, train_ids, mask,
    scores, sums,
    tf, qf, gl, g1, g2, g3, s1, s2, tmat, qmat, ot, raw, allow, cs, cr,
    g_send, g_recv, q_send, q_recv, t_send, t_recv, sib_send, sib_recv, c_send, c_recv,
):
    p, e = lax.axis_index("param"), lax.axis_index("ex")
    np_ = 2 * nz
    z, c = p // 2, p % 2
    sibling = spot(z * 2 + 1 - c, e)
    ring = (spot(lax.rem(z + 1, nz) * 2 + c, e), spot(lax.rem(z + nz - 1, nz) * 2 + c, e))
    far = nz // 2

    barrier = pltpu.get_barrier_semaphore()

    def greet(o, carry):
        pl.semaphore_signal(barrier, inc=1, device_id=spot(p, lax.rem(e + o, ne)), device_id_type=MESH)
        return carry

    def greet_column(o, carry):
        pl.semaphore_signal(barrier, inc=1, device_id=spot(lax.rem(p + o, np_), e), device_id_type=MESH)
        return carry

    lax.fori_loop(1, ne, greet, 0)
    lax.fori_loop(1, np_, greet_column, 0)

    def dot(a, b, dims=None):
        if dims is None:
            return jnp.dot(a, b, preferred_element_type=F32)
        return lax.dot_general(a, b, dims, preferred_element_type=F32)

    t_in = fac[0:T_IN, :]
    t_out = fac[T_IN:T_ALL, :]
    gi = dot(t_in, t_in, TN)
    go = dot(t_out, t_out, TN)
    gram_out = go[0:64, 0:64] + go[64:128, 64:128]
    gl[0:64, :] = gi[0:64, :]
    gl[64:128, :] = jnp.concatenate([gram_out, gi[64:128, 64:128]], axis=1)
    tf[p] = fac[0:T_ALL, :]
    pl.semaphore_wait(barrier, ne + np_ - 2)

    piece = gl.shape[0] // ne

    def plane(phase, src, dst, o):
        return remote(
            src, dst.at[e], g_send.at[phase, o], g_recv.at[phase, e], spot(p, lax.rem(e + o, ne))
        )

    def plane_from(phase, src, dst, o):
        other = lax.rem(e + ne - o, ne)
        return remote(src, dst.at[other], g_send.at[phase, o], g_recv.at[phase, other], spot(p, other))

    def column(o):
        return remote(s1, g2.at[p], g_send.at[1, o], g_recv.at[1, p], spot(lax.rem(p + o, np_), e))

    def column_from(o):
        other = lax.rem(p + np_ - o, np_)
        return remote(s1, g2.at[other], g_send.at[1, o], g_recv.at[1, other], spot(other, e))

    def part_for(o):
        start = pl.multiple_of(lax.rem(e + o, ne) * piece, piece)
        return gl.at[pl.ds(start, piece)]

    def loop(low, high, body):
        def step(i, carry):
            body(i)
            return carry

        lax.fori_loop(low, high, step, 0)

    loop(1, ne, lambda o: plane(0, part_for(o), g1, o).start())
    g1[e] = gl[pl.ds(pl.multiple_of(e * piece, piece), piece), :]

    rows_of = (pl.ds(0, T_ALL // 2), pl.ds(T_ALL // 2, T_ALL // 2))

    def owner(k):
        s = (k + 1) // 2
        return lax.rem(z + jnp.where(k % 2 == 1, nz - s, s), nz)

    def pass_on(way, step):
        s = step if way == 1 else nz - step
        block = lax.rem(z + s, nz) * 2 + c
        ref = tf.at[block] if step < far - 1 else tf.at[block, rows_of[way]]
        return remote(ref, ref, t_send.at[way, step], t_recv.at[way, step], ring[way])

    def arrival(way, step):
        s = step + 1 if way == 1 else nz - step - 1
        block = lax.rem(z + s, nz) * 2 + c
        ref = tf.at[block] if step < far - 1 else tf.at[block, rows_of[way]]
        return remote(ref, ref, t_send.at[way, step], t_recv.at[way, step], ring[way])

    def across(k, core):
        ref = tf.at[owner(k) * 2 + core]
        return remote(ref, ref, sib_send.at[k], sib_recv.at[k], sibling)

    for way in (0, 1):
        pass_on(way, 0).start()
    across(0, c).start()

    width = mask.shape[0]
    cluster_q = lax.broadcasted_iota(jnp.int32, (width, query_ids.shape[1]), 0)
    hot_q = jnp.where(cluster_q == query_ids[...], 1.0, 0.0)
    cluster_t = lax.broadcasted_iota(jnp.int32, (width, train_ids.shape[1]), 0)
    hot_t = jnp.where(cluster_t == train_ids[...], 1.0, 0.0)
    picked = dot(mask[...].astype(F32).T.astype(BF16), hot_q.astype(BF16))
    allow[...] = dot(hot_t.T.astype(BF16), picked.astype(BF16))

    def total(ref, n):
        value = ref[0]
        for i in range(1, n):
            value = value + ref[i]
        return value

    loop(1, ne, lambda o: plane_from(0, gl.at[pl.ds(0, piece)], g1, o).wait_recv())
    s1[...] = total(g1, ne)
    loop(1, np_, lambda o: column(o).start())
    g2[p] = s1[...]

    def relay(step):
        for way in (0, 1):
            arrival(way, step - 1).wait_recv()
            if step < far:
                pass_on(way, step).start()
                across(2 * step - 1 + way, c).start()
        if step == far:
            across(nz - 1, c).start()

    relay(1)
    loop(1, np_, lambda o: column_from(o).wait_recv())
    s2[...] = total(g2, np_)
    loop(1, ne, lambda o: plane(2, s2, g3, o).start())
    g3[e] = s2[...]

    q_own = fac.at[pl.ds(T_ALL, Q_ALL)]

    def q_to(o):
        return remote(q_own, qf.at[e], q_send.at[o], q_recv.at[e], spot(p, lax.rem(e + o, ne)))

    def q_from(o):
        other = lax.rem(e + ne - o, ne)
        return remote(q_own, qf.at[other], q_send.at[o], q_recv.at[other], spot(p, other))

    loop(1, ne, lambda o: q_to(o).start())
    qf[e] = fac[T_ALL:ALL, :]

    for step in range(2, far + 1):
        relay(step)
    loop(1, ne, lambda o: plane_from(2, s2, g3, o).wait_recv())
    gram = jnp.concatenate([g3[i] for i in range(ne)], axis=0)
    upper = gram[0:64, 64:128]
    gram_in = jnp.concatenate(
        [gram[0:64, :], jnp.concatenate([upper.T, gram[64:128, 64:128]], axis=1)], axis=0
    )
    inv_in = inverse_of(gram_in, count)
    inv_out = inverse_of(gram[64:128, 0:64], count)
    zero = jnp.zeros((64, 64), F32)
    both = jnp.concatenate(
        [jnp.concatenate([inv_out, zero], axis=1), jnp.concatenate([zero, inv_out], axis=1)], axis=0
    )

    def split(x):
        high = x.astype(BF16)
        return high, (x - high.astype(F32)).astype(BF16)

    lane = lax.broadcasted_iota(jnp.int32, (8, 128), 1) // 16
    own_tokens = jnp.where(lane == lax.broadcasted_iota(jnp.int32, (8, 128), 0), 1.0, 0.0)

    def spreads(row, col):
        rows = [ot[col, pl.ds(row + r, 8, stride=0), :] * own_tokens for r in range(64)]
        return jnp.concatenate(rows, axis=0).astype(BF16)

    def put(dst, t0, a, b):
        for r in range(64):
            tile = jnp.concatenate([a[8 * r : 8 * r + 8], b[8 * r : 8 * r + 8]], axis=0)
            dst[pl.ds(t0, 16), 128 * r : 128 * (r + 1)] = tile.astype(BF16)

    def form(dst, t0, first, second):
        put(dst, t0, *(dot(spreads(row, col), inputs) for row, col, inputs in (first, second)))

    def form_train(g):
        for half in (0, 1):
            ot[half] = tf[g, T_IN + 128 * half : T_IN + 128 * (half + 1), :].astype(F32).T
        for h in (0, 1):
            form(
                tmat,
                pl.multiple_of(g * 32 + 16 * h, 16),
                (64 * h, 0, tf[g, 256 * h : 256 * h + 128, :]),
                (64 * h, 1, tf[g, 256 * h + 128 : 256 * h + 256, :]),
            )

    def train_two(k):
        form_train(owner(k) * 2 + c)
        across(k, 1 - c).wait_recv()
        form_train(owner(k) * 2 + 1 - c)

    loop(0, nz, train_two)

    def thirds(x):
        high = x.astype(BF16)
        mid, low = split(x - high.astype(F32))
        return high, mid, low

    in_parts, out_parts = thirds(inv_in), thirds(both)

    def apply(a, parts):
        return dot(a, parts[0]) + (dot(a, parts[1]) + dot(a, parts[2]))

    def form_query(i):
        side = apply(qf[i, Q_IN:Q_ALL, :], out_parts).T
        side_high = side.astype(BF16).astype(F32)
        ot[0] = side_high
        ot[1] = side - side_high
        high, low = split(apply(qf[i, 0:Q_IN, :], in_parts))
        wide = jnp.concatenate([high, low], axis=1)

        def product(h):
            rows = slice(128 * h, 128 * h + 128)
            main = dot(spreads(64 * h, 0), wide[rows])
            return main[:, 0:128] + (main[:, 128:256] + dot(spreads(64 * h, 1), high[rows]))

        put(qmat, pl.multiple_of(i * 16, 16), product(0), product(1))

    form_query(e)

    def query_other(o):
        q_from(o).wait_recv()
        form_query(lax.rem(e + ne - o, ne))

    loop(1, ne, query_other)

    deep = 1024
    raw[...] = jnp.zeros_like(raw)

    def contract(i):
        at = pl.ds(pl.multiple_of(i * deep, deep), deep)
        raw[...] += dot(tmat[:, at], qmat[:, at], NT)

    loop(0, tmat.shape[1] // deep, contract)
    block = raw[...] * scale * allow[...]
    scores[...] = block
    high, low = split(block)
    hot = hot_t.astype(BF16)
    partial = (dot(hot, high) + dot(hot, low)) * spread
    share = partial.T.astype(BF16)
    rows = share.shape[0] // ne
    for i in range(ne):
        cs[i] = share[i * rows : (i + 1) * rows, :]

    def c_to(o):
        other = lax.rem(e + o, ne)
        return remote(cs.at[other], cr.at[e], c_send.at[o], c_recv.at[e], spot(p, other))

    def c_from(o):
        other = lax.rem(e + ne - o, ne)
        return remote(cs.at[other], cr.at[other], c_send.at[o], c_recv.at[other], spot(p, other))

    loop(1, ne, lambda o: c_to(o).start())
    cr[e] = cs[e]
    loop(1, ne, lambda o: c_from(o).wait_recv())
    acc = cr[0].astype(F32)
    for i in range(1, ne):
        acc = acc + cr[i].astype(F32)
    sums[...] = acc

    def drain(o):
        plane(0, part_for(o), g1, o).wait_send()
        plane(2, s2, g3, o).wait_send()
        q_to(o).wait_send()
        c_to(o).wait_send()

    loop(1, ne, drain)
    loop(1, np_, lambda o: column(o).wait_send())
    for step in range(far):
        for way in (0, 1):
            pass_on(way, step).wait_send()
    loop(0, nz, lambda k: across(k, c).wait_send())


def solution(mesh):
    np_, ne = mesh.shape["param"], mesh.shape["ex"]
    nz = np_ // 2
    far = nz // 2

    def step(qa, qg, ta, tg, win, wout, query_clusters, train_clusters, pair_mask):
        groups, q_rows, tokens, feats = qa.shape
        t_rows = ta.shape[1]
        flat = [x.reshape(x.shape[0], x.shape[1] * x.shape[2], x.shape[3]) for x in (qa, qg, ta, tg)]
        any_space = pl.BlockSpec(memory_space=pl.ANY)
        vmem = pl.BlockSpec(memory_space=pltpu.VMEM)
        dma = pltpu.SemaphoreType.DMA
        limit = 63_000_000
        fac = pl.pallas_call(
            functools.partial(reduce_kernel, nz),
            out_shape=jax.ShapeDtypeStruct((ALL, 128), BF16),
            in_specs=[any_space] * 4 + [vmem] * 2,
            out_specs=vmem,
            scratch_shapes=[
                pltpu.VMEM((groups,) + flat[0].shape[1:], BF16),
                pltpu.VMEM((groups,) + flat[1].shape[1:], BF16),
                pltpu.VMEM((groups,) + flat[2].shape[1:], BF16),
                pltpu.VMEM((groups,) + flat[3].shape[1:], BF16),
                pltpu.VMEM((2, nz, T_ALL, 128), BF16),
                pltpu.VMEM((2, nz, Q_ALL, 128), F32),
                pltpu.VMEM((nz, T_ALL, 128), BF16),
                pltpu.VMEM((nz, Q_ALL, 128), F32),
                pltpu.VMEM((2, far, T_ALL, 128), BF16),
                pltpu.VMEM((2, far, Q_ALL, 128), F32),
                pltpu.VMEM((2, far, T_ALL, 128), BF16),
                pltpu.VMEM((2, far, Q_ALL, 128), F32),
                dma((4, groups)),
                dma((2, nz)),
                dma((2, nz)),
                dma((2, far, 2, 2)),
                dma((2, far, 2, 2)),
            ],
            compiler_params=pltpu.CompilerParams(
                collective_id=0, has_side_effects=True, vmem_limit_bytes=limit
            ),
            name="reduce_factors",
        )(*flat, win, wout.T)
        all_t, all_q = groups * t_rows, q_rows * ne
        dims = win.shape[1] * wout.shape[1]
        clusters = pair_mask.shape[0]
        total = groups * t_rows * ne
        scores, sums = pl.pallas_call(
            functools.partial(
                score_kernel,
                nz,
                ne,
                float(total * tokens),
                1.0 / (tokens * math.sqrt(dims)),
                math.sqrt(clusters / total),
            ),
            out_shape=(
                jax.ShapeDtypeStruct((all_t, all_q), F32),
                jax.ShapeDtypeStruct((q_rows, clusters), F32),
            ),
            in_specs=[vmem] * 4,
            out_specs=(vmem, vmem),
            scratch_shapes=[
                pltpu.VMEM((groups, T_ALL, 128), BF16),
                pltpu.VMEM((ne, Q_ALL, 128), BF16),
                pltpu.VMEM((128, 128), F32),
                pltpu.VMEM((ne, 128 // ne, 128), F32),
                pltpu.VMEM((np_, 128 // ne, 128), F32),
                pltpu.VMEM((ne, 128 // ne, 128), F32),
                pltpu.VMEM((128 // ne, 128), F32),
                pltpu.VMEM((128 // ne, 128), F32),
                pltpu.VMEM((all_t, dims), BF16),
                pltpu.VMEM((all_q, dims), BF16),
                pltpu.VMEM((2, 128, 128), F32),
                pltpu.VMEM((all_t, all_q), F32),
                pltpu.VMEM((all_t, all_q), F32),
                pltpu.VMEM((ne, q_rows, clusters), BF16),
                pltpu.VMEM((ne, q_rows, clusters), BF16),
                dma((3, max(ne, np_))),
                dma((3, max(ne, np_))),
                dma((ne,)),
                dma((ne,)),
                dma((2, far)),
                dma((2, far)),
                dma((nz,)),
                dma((nz,)),
                dma((ne,)),
                dma((ne,)),
            ],
            compiler_params=pltpu.CompilerParams(
                collective_id=1, has_side_effects=True, vmem_limit_bytes=limit
            ),
            name="score",
        )(fac, query_clusters, train_clusters.reshape(1, -1), pair_mask)
        return (
            scores.T.reshape(1, all_q, groups, t_rows),
            sums.reshape(1, q_rows, clusters),
        )

    return jax.shard_map(
        step,
        mesh=mesh,
        in_specs=(
            P(None, "ex", None, "param"),
            P(None, "ex", None, "param"),
            P(None, "ex", None, "param"),
            P(None, "ex", None, "param"),
            P("param", None),
            P("param", None),
            P("param", None),
            P(None, "ex"),
            P(),
        ),
        out_specs=(P("param", None, None, "ex"), P("param", "ex", None)),
        check_vma=False,
    )
```

time: 643 us -> 118 us (0.18)
  waiting for transfers between devices: 436 us -> 0 us
  Pallas kernels: 0 us -> 112 us
  blocking collectives: 75.2 us -> 0 us
  other arithmetic: 57.3 us -> 0 us
  local copies, waits for them, and re-layouts: 38.8 us -> 4.53 us
  matrix products: 19.1 us -> 0 us
  between operations: 16 us -> 0.65 us
    psum x1 -> x0, waiting for transfers between devices: 155 us -> none  [shards(): gram_in, gram_out = lax.psum((gram_in, gram_out), ('param', 'ex'))]
    pallas_call x0 -> x2, Pallas kernels: none -> 112 us  [the longest x1 66.7 us: step(): pl.pallas_call(functools.partial(score_kernel, nz, ne, float(total * toke...]
    all_gather x2 -> x0, waiting for transfers between devices: 110 us -> none  [the longest x1 57.9 us: shards(): lax.all_gather(form_grads(train_out, train_in), 'param', axis=0, tiled=True)]
    unnamed x6 -> x0, waiting for transfers between devices: 88.3 us -> none
    reduce_scatter x1 -> x0, waiting for transfers between devices: 82.4 us -> none  [shards(): lax.psum_scatter(jnp.concatenate(pieces, axis=1), 'param', scatter_dimens...]
    psum x1 -> x0, blocking collectives: 75.2 us -> none  [shards(): gram_in, gram_out = lax.psum((gram_in, gram_out), ('param', 'ex'))]
    another operation x10 -> x0, other arithmetic: 34.9 us -> none  [the longest x6 18.9 us: inverse_of(): factor = jnp.linalg.cholesky(mean + damping * identity)]
    reshape x2 -> x1, local copies, waits for them, and re-layouts: 20.5 us -> 1.35 us  [step(): train_clusters.reshape(1, -1)]
  transfers between devices with their start and end apart: 5 -> 0, of which waited for: 5 -> 0; matrix products, arithmetic and copies ran while one was open for 3% -> 0% of each run, Pallas kernels for 0% -> 0%
where the time goes in v1:
time: 118 us; the launch traced here: 117 us
  Pallas kernels  112 us (95%)
  local copies, waits for them, and re-layouts  4.53 us (4%)
    pallas_call x1, Pallas kernels, step(): pl.pallas_call(functools.partial(score_kernel, nz, ne, float(total * toke...  66.7 us
    pallas_call x1, Pallas kernels, step(): pl.pallas_call(functools.partial(reduce_kernel, nz), out_shape=jax.ShapeD...  45 us
    unnamed x2, local copies, waits for them, and re-layouts  3.18 us

profile of v1, /device:TPU:2, one launch (start us, length us, event | category | flops | bytes accessed | tf_op | source)
XLA Modules:
  0.0 116.9 jit_solution(15062101006948162987)
XLA Ops:
  0.6 1.4 %reshape.29.train_ids = s32[1,512]{1,0:T(1,128)} reshape(s32[16,32]{1,0:T(8,128)} %param.16) | data formatting | bytes 4096 | tf_op jit(solution)/shard_map/reshape | solution.py:598
  2.0 45.0 %reduce_factors.1.fac = bf16[1152,128]{1,0:T(8,128)(2,1)} custom-call(bf16[16,256,256]{2,1,0:T(8,128)(2,1)} %bitcast.11, bf16[16,256,256]{2,1,0:T(8,128)(2,1)} %bitcast.12, bf16[16,512,256]{2,1,0:T(8,128)(2,1)} %bitcast.9, bf16[16,512,256]{2,1,0:T(8,128)(2,1)} %bitcast.10, bf16[256,128]{1,0:T(8,128)(2,1)} %win.1, bf16[64,256]{1,0:T(8,128)(2,1)} %bitcast.14), custom_call_target="tpu_custom_call" | custom-call | tf_op jit(solution)/shard_map/reduce_factors/pallas_call | solution.py:519
  47.0 66.7 %score.1 = (f32[512,256]{1,0:T(8,128)}, f32[16,128]{1,0:T(8,128)}) custom-call(bf16[1152,128]{1,0:T(8,128)(2,1)} %reduce_factors.1.fac, s32[1,256]{1,0:T(1,128)} %query_ids.1, s32[1,512]{1,0:T(1,128)} %reshape.29.train_ids, s32[128,128]{1,0:T(8,128)} %mask.1), custom_call_target="tpu_custom_call" | custom-call | tf_op jit(solution)/shard_map/score/pallas_call | solution.py:552
  113.7 1.9 %copy.13 = f32[1,256,16,32]{1,3,2,0:T(8,128)} copy(f32[1,256,16,32]{1,3,2,0:T(8,128)} %bitcast.13) | data formatting | bytes 1048576
  115.6 1.3 %copy.14 = f32[1,16,128]{2,1,0:T(8,128)} copy(f32[1,16,128]{2,1,0:T(8,128)} %bitcast.15) | data formatting | bytes 16384

commit v2 on v1

--- a/solution.py
+++ b/solution.py
@@ -324,6 +324,48 @@
         pass_on(way, 0).start()
     across(0, c).start()
 
+    edge = math.isqrt(ne)
+    half = Q_ALL // 2
+
+    def place(o, da, db):
+        a, b = (e // edge, e % edge) if o == 0 else (e % edge, e // edge)
+        a, b = lax.rem(a + da + edge, edge), lax.rem(b + db + edge, edge)
+        return a * edge + b if o == 0 else b * edge + a
+
+    along = (0, -1, 1, 2)
+
+    def q_copy(o, way, slot, sending):
+        back = 0 if sending else (-1 if way == 0 else 1)
+        sign = 1 if way == 0 else -1
+        rows = pl.ds(half * o, half)
+        if slot == 0:
+            block, target = place(o, back, 0), place(o, sign, 0)
+        elif slot == 1:
+            block, target = place(o, back - sign, 0), place(o, sign, 0)
+            rows = pl.ds(half * o + half // 2 * way, half // 2)
+        elif slot < 6:
+            block, target = place(o, along[slot - 2], back), place(o, 0, sign)
+        else:
+            block, target = place(o, along[2 * way + slot - 6], back - sign), place(o, 0, sign)
+        ref = qf.at[block, rows]
+        return remote(ref, ref, q_send.at[o, way, slot], q_recv.at[o, way, slot], spot(p, target))
+
+    both_ways = [(o, way) for o in (0, 1) for way in (0, 1)]
+
+    def q_start(*slots):
+        for slot in slots:
+            for o, way in both_ways:
+                q_copy(o, way, slot, True).start()
+
+    def q_wait(*slots):
+        for slot in slots:
+            for o, way in both_ways:
+                q_copy(o, way, slot, False).wait_recv()
+
+    qf[e] = fac[T_ALL:ALL, :]
+
+    q_start(0, 2)
+
     width = mask.shape[0]
     cluster_q = lax.broadcasted_iota(jnp.int32, (width, query_ids.shape[1]), 0)
     hot_q = jnp.where(cluster_q == query_ids[...], 1.0, 0.0)
@@ -352,25 +394,23 @@
         if step == far:
             across(nz - 1, c).start()
 
+    q_wait(0)
+    q_start(1, 3, 4)
     relay(1)
+    q_wait(1)
+    q_start(5)
     loop(1, np_, lambda o: column_from(o).wait_recv())
     s2[...] = total(g2, np_)
     loop(1, ne, lambda o: plane(2, s2, g3, o).start())
     g3[e] = s2[...]
 
-    q_own = fac.at[pl.ds(T_ALL, Q_ALL)]
-
-    def q_to(o):
-        return remote(q_own, qf.at[e], q_send.at[o], q_recv.at[e], spot(p, lax.rem(e + o, ne)))
-
-    def q_from(o):
-        other = lax.rem(e + ne - o, ne)
-        return remote(q_own, qf.at[other], q_send.at[o], q_recv.at[other], spot(p, other))
-
-    loop(1, ne, lambda o: q_to(o).start())
-    qf[e] = fac[T_ALL:ALL, :]
-
-    for step in range(2, far + 1):
+    relay(2)
+    for o in (0, 1):
+        for way in (0, 1):
+            for index in (0, 1):
+                q_copy(o, way, 2 + 2 * way + index, False).wait_recv()
+                q_copy(o, way, 6 + index, True).start()
+    for step in range(3, far + 1):
         relay(step)
     loop(1, ne, lambda o: plane_from(2, s2, g3, o).wait_recv())
     gram = jnp.concatenate([g3[i] for i in range(ne)], axis=0)
@@ -447,13 +487,11 @@
 
         put(qmat, pl.multiple_of(i * 16, 16), product(0), product(1))
 
-    form_query(e)
-
-    def query_other(o):
-        q_from(o).wait_recv()
-        form_query(lax.rem(e + ne - o, ne))
-
-    loop(1, ne, query_other)
+    for o in (0, 1):
+        for way in (0, 1):
+            for slot in (4 - 2 * way, 5 - 2 * way, 6, 7):
+                q_copy(o, way, slot, False).wait_recv()
+    loop(0, ne, form_query)
 
     deep = 1024
     raw[...] = jnp.zeros_like(raw)
@@ -492,10 +530,12 @@
     def drain(o):
         plane(0, part_for(o), g1, o).wait_send()
         plane(2, s2, g3, o).wait_send()
-        q_to(o).wait_send()
         c_to(o).wait_send()
 
     loop(1, ne, drain)
+    for o, way in both_ways:
+        for slot in range(8):
+            q_copy(o, way, slot, True).wait_send()
     loop(1, np_, lambda o: column(o).wait_send())
     for step in range(far):
         for way in (0, 1):
@@ -582,8 +622,8 @@
                 pltpu.VMEM((ne, q_rows, clusters), BF16),
                 dma((3, max(ne, np_))),
                 dma((3, max(ne, np_))),
-                dma((ne,)),
-                dma((ne,)),
+                dma((2, 2, 8)),
+                dma((2, 2, 8)),
                 dma((2, far)),
                 dma((2, far)),
                 dma((nz,)),

time: 118 us -> 112 us (0.949)
  Pallas kernels: 112 us -> 106 us
    pallas_call x1, Pallas kernels: 66.7 us -> 61 us  [step(): pl.pallas_call(functools.partial(score_kernel, nz, ne, float(total * toke...]
where the time goes in v2:
time: 112 us; the launch traced here: 111 us
  Pallas kernels  106 us (95%)
  local copies, waits for them, and re-layouts  4.53 us (4%)
    pallas_call x1, Pallas kernels, step(): pl.pallas_call(functools.partial(score_kernel, nz, ne, float(total * toke...  61 us
    pallas_call x1, Pallas kernels, step(): pl.pallas_call(functools.partial(reduce_kernel, nz), out_shape=jax.ShapeD...  45 us
    unnamed x2, local copies, waits for them, and re-layouts  3.18 us

profile of v2, /device:TPU:2, one launch (start us, length us, event | category | flops | bytes accessed | tf_op | source)
XLA Modules:
  0.0 111.2 jit_solution(7631579078688756579)
XLA Ops:
  0.6 1.4 %reshape.29.train_ids = s32[1,512]{1,0:T(1,128)} reshape(s32[16,32]{1,0:T(8,128)} %param.16) | data formatting | bytes 4096 | tf_op jit(solution)/shard_map/reshape | solution.py:638
  2.0 45.0 %reduce_factors.1.fac = bf16[1152,128]{1,0:T(8,128)(2,1)} custom-call(bf16[16,256,256]{2,1,0:T(8,128)(2,1)} %bitcast.11, bf16[16,256,256]{2,1,0:T(8,128)(2,1)} %bitcast.12, bf16[16,512,256]{2,1,0:T(8,128)(2,1)} %bitcast.9, bf16[16,512,256]{2,1,0:T(8,128)(2,1)} %bitcast.10, bf16[256,128]{1,0:T(8,128)(2,1)} %win.1, bf16[64,256]{1,0:T(8,128)(2,1)} %bitcast.14), custom_call_target="tpu_custom_call" | custom-call | tf_op jit(solution)/shard_map/reduce_factors/pallas_call | solution.py:559
  47.0 61.0 %score.1 = (f32[512,256]{1,0:T(8,128)}, f32[16,128]{1,0:T(8,128)}) custom-call(bf16[1152,128]{1,0:T(8,128)(2,1)} %reduce_factors.1.fac, s32[1,256]{1,0:T(1,128)} %query_ids.1, s32[1,512]{1,0:T(1,128)} %reshape.29.train_ids, s32[128,128]{1,0:T(8,128)} %mask.1), custom_call_target="tpu_custom_call" | custom-call | tf_op jit(solution)/shard_map/score/pallas_call | solution.py:592
  108.0 1.9 %copy.13 = f32[1,256,16,32]{1,3,2,0:T(8,128)} copy(f32[1,256,16,32]{1,3,2,0:T(8,128)} %bitcast.13) | data formatting | bytes 1048576
  109.9 1.3 %copy.14 = f32[1,16,128]{2,1,0:T(8,128)} copy(f32[1,16,128]{2,1,0:T(8,128)} %bitcast.15) | data formatting | bytes 16384

commit v3 on v2

--- a/solution.py
+++ b/solution.py
@@ -34,14 +34,59 @@
     return (pl.ds(0, size), pl.ds(size, size))
 
 
-def reduce_kernel(
-    nz,
-    qa, qg, ta, tg, win, wout,
-    out,
+def newton(damped, level, steps, scalings):
+    size = damped.shape[0]
+    rows = lax.broadcasted_iota(jnp.int32, (size, size), 0)
+    eye = (rows == lax.broadcasted_iota(jnp.int32, (size, size), 1)).astype(F32)
+
+    def dot(a, b):
+        return jnp.dot(a, b, preferred_element_type=F32, precision=lax.Precision.HIGHEST)
+
+    resid = eye - level * damped
+    guess = level * eye
+    for index in range(steps):
+        c = scalings[index]
+        grown = guess + (level * resid if index == 0 else dot(guess, resid))
+        resid = (1.0 - c) * eye + c * dot(resid, resid)
+        guess = c * grown
+    for _ in range(2):
+        resid = eye - dot(damped, guess)
+        guess = guess + dot(guess, resid)
+    return 0.5 * (guess + guess.T)
+
+
+def schedule_of(size):
+    kappa = 1.0 + 10.0 * size
+    rho = (kappa - 1.0) / (kappa + 1.0)
+    scalings = []
+    while rho > 1e-4:
+        scalings.append(2.0 / (2.0 - rho * rho))
+        rho = rho * rho / (2.0 - rho * rho)
+    return 2.0 / (1.0 + kappa), scalings
+
+
+def inverse_of(gram, count):
+    size = gram.shape[0]
+    mean = gram * (1.0 / count)
+    rows = lax.broadcasted_iota(jnp.int32, (size, size), 0)
+    diagonal = rows == lax.broadcasted_iota(jnp.int32, (size, size), 1)
+    floor = 0.1 / size * jnp.sum(jnp.where(diagonal, mean, 0.0), keepdims=True)
+    damped = mean + jnp.where(diagonal, floor, 0.0)
+    level, scalings = schedule_of(size)
+    return newton(damped, level / floor, len(scalings), scalings)
+
+
+def kernel(
+    nz, ne, count, scale, spread,
+    qa, qg, ta, tg, win, wout, query_ids, train_ids, mask,
+    scores, sums,
     qa_b, qg_b, ta_b, tg_b, part_t, part_q, sib_t, sib_q, snd_t, snd_q, rcv_t, rcv_q,
+    tf, qf, gl, g1, g2, g3, s1, s2, tmat, qmat, ot, raw, allow, cs, cr,
     in_sem, sib_send, sib_recv, ring_send, ring_recv,
+    g_send, g_recv, q_send, q_recv, t_send, t_recv, over_send, over_recv, c_send, c_recv,
 ):
     p, e = lax.axis_index("param"), lax.axis_index("ex")
+    np_ = 2 * nz
     z, c = p // 2, p % 2
     sibling = spot(z * 2 + 1 - c, e)
     ring = (spot(lax.rem(z + 1, nz) * 2 + c, e), spot(lax.rem(z + nz - 1, nz) * 2 + c, e))
@@ -72,18 +117,38 @@
 
     lax.fori_loop(0, 2 * nz, start, 0)
     barrier = pltpu.get_barrier_semaphore()
-    for device in (sibling,) + ring:
-        pl.semaphore_signal(barrier, inc=1, device_id=device, device_id_type=MESH)
-    pl.semaphore_wait(barrier, 3)
+
+    def greet(o, carry):
+        pl.semaphore_signal(barrier, inc=1, device_id=spot(p, lax.rem(e + o, ne)), device_id_type=MESH)
+        return carry
+
+    def greet_column(o, carry):
+        pl.semaphore_signal(barrier, inc=1, device_id=spot(lax.rem(p + o, np_), e), device_id_type=MESH)
+        return carry
+
+    lax.fori_loop(1, ne, greet, 0)
+    lax.fori_loop(1, np_, greet_column, 0)
+
+    def dot(a, b, dims=None):
+        if dims is None:
+            return jnp.dot(a, b, preferred_element_type=F32)
+        return lax.dot_general(a, b, dims, preferred_element_type=F32)
+
+    width = mask.shape[0]
+    cluster_q = lax.broadcasted_iota(jnp.int32, (width, query_ids.shape[1]), 0)
+    hot_q = jnp.where(cluster_q == query_ids[...], 1.0, 0.0)
+    cluster_t = lax.broadcasted_iota(jnp.int32, (width, train_ids.shape[1]), 0)
+    hot_t = jnp.where(cluster_t == train_ids[...], 1.0, 0.0)
+    picked = dot(mask[...].astype(F32).T.astype(BF16), hot_q.astype(BF16))
+    allow[...] = dot(hot_t.T.astype(BF16), picked.astype(BF16))
+
+    pl.semaphore_wait(barrier, ne + np_ - 2)
 
     w_in = win[...]
     narrow = wout[...].astype(F32).T
     blank = jnp.zeros_like(narrow)
     w_low = jnp.concatenate([narrow, blank], axis=1).astype(BF16)
     w_high = jnp.concatenate([blank, narrow], axis=1).astype(BF16)
-
-    def dot(a, b):
-        return jnp.dot(a, b, preferred_element_type=F32)
 
     parts, sibs, sends, recvs = (part_t, part_q), (sib_t, sib_q), (snd_t, snd_q), (rcv_t, rcv_q)
 
@@ -141,130 +206,22 @@
         copy.start()
         hops.append(copy)
 
-    def round_of(step, chunk):
-        if step == 0:
-            for way in (0, 1):
-                send(way, 0, chunk, way)
-            return
-        for late in (1, 0):
-            for way in (0, 1):
-                send(way, step, chunk, way if late == 0 else 1 - way)
-
-    for step in range(far):
-        low, high = (0, 2) if step == 0 else (4 * step - 2, 4 * step + 2)
-        lax.fori_loop(low, high, project, 0)
-        for k in range(low // 2, high // 2):
-            to_sibling(k, 0).wait_recv()
-            to_sibling(k, 1).wait_recv()
-        round_of(step, 0)
-    round_of(0, 1)
-    lax.fori_loop(2 * nz - 2, 2 * nz, project, 0)
-    to_sibling(nz - 1, 0).wait_recv()
-    to_sibling(nz - 1, 1).wait_recv()
-
-    def final(chunk):
-        for half in (1, 0):
-            rows = halves(chunk)[half]
+    def short(step, chunk):
+        for way in (0, 1):
+            send(way, step, chunk, 1 - way)
+
+    def long(step, chunk):
+        for way in (0, 1):
+            send(way, step, chunk, way)
+
+    def final(chunk, put):
+        for index in (1, 0):
+            rows = halves(chunk)[index]
             value = own_sum(nz - 1, chunk, rows)
             for way in (0, 1):
-                hop(way, far - 1, chunk, half).wait_recv()
+                hop(way, far - 1, chunk, index).wait_recv()
                 value = value + recvs[chunk][way, far - 1, rows, :].astype(F32)
-            out[pl.ds(T_ALL * chunk + rows.start, rows.size), :] = value.astype(BF16)
-
-    for step in range(1, far):
-        round_of(step, 1)
-    final(0)
-    final(1)
-    for copy in hops:
-        copy.wait_send()
-    for k in range(nz):
-        to_sibling(k, 0).wait_send()
-        to_sibling(k, 1).wait_send()
-
-
-def newton(damped, level, steps, scalings):
-    size = damped.shape[0]
-    rows = lax.broadcasted_iota(jnp.int32, (size, size), 0)
-    eye = (rows == lax.broadcasted_iota(jnp.int32, (size, size), 1)).astype(F32)
-
-    def dot(a, b):
-        return jnp.dot(a, b, preferred_element_type=F32, precision=lax.Precision.HIGHEST)
-
-    resid = eye - level * damped
-    guess = level * eye
-    for index in range(steps):
-        c = scalings[index]
-        grown = guess + (level * resid if index == 0 else dot(guess, resid))
-        resid = (1.0 - c) * eye + c * dot(resid, resid)
-        guess = c * grown
-    for _ in range(2):
-        resid = eye - dot(damped, guess)
-        guess = guess + dot(guess, resid)
-    return 0.5 * (guess + guess.T)
-
-
-def schedule_of(size):
-    kappa = 1.0 + 10.0 * size
-    rho = (kappa - 1.0) / (kappa + 1.0)
-    scalings = []
-    while rho > 1e-4:
-        scalings.append(2.0 / (2.0 - rho * rho))
-        rho = rho * rho / (2.0 - rho * rho)
-    return 2.0 / (1.0 + kappa), scalings
-
-
-def inverse_of(gram, count):
-    size = gram.shape[0]
-    mean = gram * (1.0 / count)
-    rows = lax.broadcasted_iota(jnp.int32, (size, size), 0)
-    diagonal = rows == lax.broadcasted_iota(jnp.int32, (size, size), 1)
-    floor = 0.1 / size * jnp.sum(jnp.where(diagonal, mean, 0.0), keepdims=True)
-    damped = mean + jnp.where(diagonal, floor, 0.0)
-    level, scalings = schedule_of(size)
-    return newton(damped, level / floor, len(scalings), scalings)
-
-
-def score_kernel(
-    nz, ne, count, scale, spread,
-    fac, query_ids, train_ids, mask,
-    scores, sums,
-    tf, qf, gl, g1, g2, g3, s1, s2, tmat, qmat, ot, raw, allow, cs, cr,
-    g_send, g_recv, q_send, q_recv, t_send, t_recv, sib_send, sib_recv, c_send, c_recv,
-):
-    p, e = lax.axis_index("param"), lax.axis_index("ex")
-    np_ = 2 * nz
-    z, c = p // 2, p % 2
-    sibling = spot(z * 2 + 1 - c, e)
-    ring = (spot(lax.rem(z + 1, nz) * 2 + c, e), spot(lax.rem(z + nz - 1, nz) * 2 + c, e))
-    far = nz // 2
-
-    barrier = pltpu.get_barrier_semaphore()
-
-    def greet(o, carry):
-        pl.semaphore_signal(barrier, inc=1, device_id=spot(p, lax.rem(e + o, ne)), device_id_type=MESH)
-        return carry
-
-    def greet_column(o, carry):
-        pl.semaphore_signal(barrier, inc=1, device_id=spot(lax.rem(p + o, np_), e), device_id_type=MESH)
-        return carry
-
-    lax.fori_loop(1, ne, greet, 0)
-    lax.fori_loop(1, np_, greet_column, 0)
-
-    def dot(a, b, dims=None):
-        if dims is None:
-            return jnp.dot(a, b, preferred_element_type=F32)
-        return lax.dot_general(a, b, dims, preferred_element_type=F32)
-
-    t_in = fac[0:T_IN, :]
-    t_out = fac[T_IN:T_ALL, :]
-    gi = dot(t_in, t_in, TN)
-    go = dot(t_out, t_out, TN)
-    gram_out = go[0:64, 0:64] + go[64:128, 64:128]
-    gl[0:64, :] = gi[0:64, :]
-    gl[64:128, :] = jnp.concatenate([gram_out, gi[64:128, 64:128]], axis=1)
-    tf[p] = fac[0:T_ALL, :]
-    pl.semaphore_wait(barrier, ne + np_ - 2)
+            put(rows, value.astype(BF16))
 
     piece = gl.shape[0] // ne
 
@@ -294,9 +251,6 @@
             return carry
 
         lax.fori_loop(low, high, step, 0)
-
-    loop(1, ne, lambda o: plane(0, part_for(o), g1, o).start())
-    g1[e] = gl[pl.ds(pl.multiple_of(e * piece, piece), piece), :]
 
     rows_of = (pl.ds(0, T_ALL // 2), pl.ds(T_ALL // 2, T_ALL // 2))
 
@@ -318,11 +272,7 @@
 
     def across(k, core):
         ref = tf.at[owner(k) * 2 + core]
-        return remote(ref, ref, sib_send.at[k], sib_recv.at[k], sibling)
-
-    for way in (0, 1):
-        pass_on(way, 0).start()
-    across(0, c).start()
+        return remote(ref, ref, over_send.at[k], over_recv.at[k], sibling)
 
     edge = math.isqrt(ne)
     half = Q_ALL // 2
@@ -362,28 +312,11 @@
             for o, way in both_ways:
                 q_copy(o, way, slot, False).wait_recv()
 
-    qf[e] = fac[T_ALL:ALL, :]
-
-    q_start(0, 2)
-
-    width = mask.shape[0]
-    cluster_q = lax.broadcasted_iota(jnp.int32, (width, query_ids.shape[1]), 0)
-    hot_q = jnp.where(cluster_q == query_ids[...], 1.0, 0.0)
-    cluster_t = lax.broadcasted_iota(jnp.int32, (width, train_ids.shape[1]), 0)
-    hot_t = jnp.where(cluster_t == train_ids[...], 1.0, 0.0)
-    picked = dot(mask[...].astype(F32).T.astype(BF16), hot_q.astype(BF16))
-    allow[...] = dot(hot_t.T.astype(BF16), picked.astype(BF16))
-
     def total(ref, n):
         value = ref[0]
         for i in range(1, n):
             value = value + ref[i]
         return value
-
-    loop(1, ne, lambda o: plane_from(0, gl.at[pl.ds(0, piece)], g1, o).wait_recv())
-    s1[...] = total(g1, ne)
-    loop(1, np_, lambda o: column(o).start())
-    g2[p] = s1[...]
 
     def relay(step):
         for way in (0, 1):
@@ -394,25 +327,105 @@
         if step == far:
             across(nz - 1, c).start()
 
-    q_wait(0)
-    q_start(1, 3, 4)
-    relay(1)
-    q_wait(1)
-    q_start(5)
+    def split(x):
+        high = x.astype(BF16)
+        return high, (x - high.astype(F32)).astype(BF16)
+
+    lane = lax.broadcasted_iota(jnp.int32, (8, 128), 1) // 16
+    own_tokens = jnp.where(lane == lax.broadcasted_iota(jnp.int32, (8, 128), 0), 1.0, 0.0)
+
+    def spreads(row, col):
+        rows = [ot[col, pl.ds(row + r, 8, stride=0), :] * own_tokens for r in range(64)]
+        return jnp.concatenate(rows, axis=0).astype(BF16)
+
+    def put(dst, t0, a, b):
+        for r in range(64):
+            tile = jnp.concatenate([a[8 * r : 8 * r + 8], b[8 * r : 8 * r + 8]], axis=0)
+            dst[pl.ds(t0, 16), 128 * r : 128 * (r + 1)] = tile.astype(BF16)
+
+    def form(dst, t0, first, second):
+        put(dst, t0, *(dot(spreads(row, col), inputs) for row, col, inputs in (first, second)))
+
+    def form_train(g):
+        for half in (0, 1):
+            ot[half] = tf[g, T_IN + 128 * half : T_IN + 128 * (half + 1), :].astype(F32).T
+        for h in (0, 1):
+            form(
+                tmat,
+                pl.multiple_of(g * 32 + 16 * h, 16),
+                (64 * h, 0, tf[g, 256 * h : 256 * h + 128, :]),
+                (64 * h, 1, tf[g, 256 * h + 128 : 256 * h + 256, :]),
+            )
+
+    def form_trains(low, high):
+        def one(u):
+            k, own = u // 2, u % 2
+            core = jnp.where(own == 0, c, 1 - c)
+
+            @pl.when(own == 1)
+            def _():
+                across(k, 1 - c).wait_recv()
+
+            form_train(owner(k) * 2 + core)
+
+        loop(low, high, one)
+
+    for step in range(far):
+        low, high = (0, 2) if step == 0 else (4 * step - 2, 4 * step + 2)
+        lax.fori_loop(low, high, project, 0)
+        for k in range(low // 2, high // 2):
+            to_sibling(k, 0).wait_recv()
+            to_sibling(k, 1).wait_recv()
+        if step:
+            short(step, 0)
+        long(step, 0)
+    long(0, 1)
+    short(1, 1)
+    lax.fori_loop(2 * nz - 2, 2 * nz, project, 0)
+    to_sibling(nz - 1, 0).wait_recv()
+    to_sibling(nz - 1, 1).wait_recv()
+
+    def put_train(rows, value):
+        tf[p, rows, :] = value
+
+    def put_query(rows, value):
+        qf[e, rows, :] = value
+
+    final(0, put_train)
+
+    def gram_local():
+        t_in = tf[p, 0:T_IN, :]
+        t_out = tf[p, T_IN:T_ALL, :]
+        gi = dot(t_in, t_in, TN)
+        go = dot(t_out, t_out, TN)
+        gram_out = go[0:64, 0:64] + go[64:128, 64:128]
+        gl[0:64, :] = gi[0:64, :]
+        gl[64:128, :] = jnp.concatenate([gram_out, gi[64:128, 64:128]], axis=1)
+
+    gram_local()
+    loop(1, ne, lambda o: plane(0, part_for(o), g1, o).start())
+    g1[e] = gl[pl.ds(pl.multiple_of(e * piece, piece), piece), :]
+    long(1, 1)
+    form_trains(0, 1)
+    loop(1, ne, lambda o: plane_from(0, gl.at[pl.ds(0, piece)], g1, o).wait_recv())
+    s1[...] = total(g1, ne)
+    loop(1, np_, lambda o: column(o).start())
+    g2[p] = s1[...]
+    short(2, 1)
+    long(2, 1)
+    for way in (0, 1):
+        pass_on(way, 0).start()
+    across(0, c).start()
     loop(1, np_, lambda o: column_from(o).wait_recv())
     s2[...] = total(g2, np_)
     loop(1, ne, lambda o: plane(2, s2, g3, o).start())
     g3[e] = s2[...]
-
-    relay(2)
-    for o in (0, 1):
-        for way in (0, 1):
-            for index in (0, 1):
-                q_copy(o, way, 2 + 2 * way + index, False).wait_recv()
-                q_copy(o, way, 6 + index, True).start()
-    for step in range(3, far + 1):
-        relay(step)
+    for step in range(3, far):
+        short(step, 1)
+        long(step, 1)
+    form_trains(1, 2)
     loop(1, ne, lambda o: plane_from(2, s2, g3, o).wait_recv())
+    relay(1)
     gram = jnp.concatenate([g3[i] for i in range(ne)], axis=0)
     upper = gram[0:64, 64:128]
     gram_in = jnp.concatenate(
@@ -425,42 +438,22 @@
         [jnp.concatenate([inv_out, zero], axis=1), jnp.concatenate([zero, inv_out], axis=1)], axis=0
     )
 
-    def split(x):
-        high = x.astype(BF16)
-        return high, (x - high.astype(F32)).astype(BF16)
-
-    lane = lax.broadcasted_iota(jnp.int32, (8, 128), 1) // 16
-    own_tokens = jnp.where(lane == lax.broadcasted_iota(jnp.int32, (8, 128), 0), 1.0, 0.0)
-
-    def spreads(row, col):
-        rows = [ot[col, pl.ds(row + r, 8, stride=0), :] * own_tokens for r in range(64)]
-        return jnp.concatenate(rows, axis=0).astype(BF16)
-
-    def put(dst, t0, a, b):
-        for r in range(64):
-            tile = jnp.concatenate([a[8 * r : 8 * r + 8], b[8 * r : 8 * r + 8]], axis=0)
-            dst[pl.ds(t0, 16), 128 * r : 128 * (r + 1)] = tile.astype(BF16)
-
-    def form(dst, t0, first, second):
-        put(dst, t0, *(dot(spreads(row, col), inputs) for row, col, inputs in (first, second)))
-
-    def form_train(g):
-        for half in (0, 1):
-            ot[half] = tf[g, T_IN + 128 * half : T_IN + 128 * (half + 1), :].astype(F32).T
-        for h in (0, 1):
-            form(
-                tmat,
-                pl.multiple_of(g * 32 + 16 * h, 16),
-                (64 * h, 0, tf[g, 256 * h : 256 * h + 128, :]),
-                (64 * h, 1, tf[g, 256 * h + 128 : 256 * h + 256, :]),
-            )
-
-    def train_two(k):
-        form_train(owner(k) * 2 + c)
-        across(k, 1 - c).wait_recv()
-        form_train(owner(k) * 2 + 1 - c)
-
-    loop(0, nz, train_two)
+    final(1, put_query)
+    q_start(0, 2)
+    form_trains(2, 6)
+    q_wait(0)
+    q_start(1, 3, 4)
+    relay(2)
+    q_wait(1)
+    q_start(5)
+    form_trains(6, 10)
+    for o, way in both_ways:
+        for index in (0, 1):
+            q_copy(o, way, 2 + 2 * way + index, False).wait_recv()
+            q_copy(o, way, 6 + index, True).start()
+    for step in range(3, far + 1):
+        relay(step)
+    form_trains(10, 2 * nz)
 
     def thirds(x):
         high = x.astype(BF16)
@@ -487,10 +480,9 @@
 
         put(qmat, pl.multiple_of(i * 16, 16), product(0), product(1))
 
-    for o in (0, 1):
-        for way in (0, 1):
-            for slot in (4 - 2 * way, 5 - 2 * way, 6, 7):
-                q_copy(o, way, slot, False).wait_recv()
+    for o, way in both_ways:
+        for slot in (4 - 2 * way, 5 - 2 * way, 6, 7):
+            q_copy(o, way, slot, False).wait_recv()
     loop(0, ne, form_query)
 
     deep = 1024
@@ -541,6 +533,11 @@
         for way in (0, 1):
             pass_on(way, step).wait_send()
     loop(0, nz, lambda k: across(k, c).wait_send())
+    for copy in hops:
+        copy.wait_send()
+    for k in range(nz):
+        to_sibling(k, 0).wait_send()
+        to_sibling(k, 1).wait_send()
 
 
 def solution(mesh):
@@ -556,11 +553,25 @@
         vmem = pl.BlockSpec(memory_space=pltpu.VMEM)
         dma = pltpu.SemaphoreType.DMA
         limit = 63_000_000
-        fac = pl.pallas_call(
-            functools.partial(reduce_kernel, nz),
-            out_shape=jax.ShapeDtypeStruct((ALL, 128), BF16),
-            in_specs=[any_space] * 4 + [vmem] * 2,
-            out_specs=vmem,
+        all_t, all_q = groups * t_rows, q_rows * ne
+        dims = win.shape[1] * wout.shape[1]
+        clusters = pair_mask.shape[0]
+        total = groups * t_rows * ne
+        scores, sums = pl.pallas_call(
+            functools.partial(
+                kernel,
+                nz,
+                ne,
+                float(total * tokens),
+                1.0 / (tokens * math.sqrt(dims)),
+                math.sqrt(clusters / total),
+            ),
+            out_shape=(
+                jax.ShapeDtypeStruct((all_t, all_q), F32),
+                jax.ShapeDtypeStruct((q_rows, clusters), F32),
+            ),
+            in_specs=[any_space] * 4 + [vmem] * 5,
+            out_specs=(vmem, vmem),
             scratch_shapes=[
                 pltpu.VMEM((groups,) + flat[0].shape[1:], BF16),
                 pltpu.VMEM((groups,) + flat[1].shape[1:], BF16),
@@ -574,37 +585,6 @@
                 pltpu.VMEM((2, far, Q_ALL, 128), F32),
                 pltpu.VMEM((2, far, T_ALL, 128), BF16),
                 pltpu.VMEM((2, far, Q_ALL, 128), F32),
-                dma((4, groups)),
-                dma((2, nz)),
-                dma((2, nz)),
-                dma((2, far, 2, 2)),
-                dma((2, far, 2, 2)),
-            ],
-            compiler_params=pltpu.CompilerParams(
-                collective_id=0, has_side_effects=True, vmem_limit_bytes=limit
-            ),
-            name="reduce_factors",
-        )(*flat, win, wout.T)
-        all_t, all_q = groups * t_rows, q_rows * ne
-        dims = win.shape[1] * wout.shape[1]
-        clusters = pair_mask.shape[0]
-        total = groups * t_rows * ne
-        scores, sums = pl.pallas_call(
-            functools.partial(
-                score_kernel,
-                nz,
-                ne,
-                float(total * tokens),
-                1.0 / (tokens * math.sqrt(dims)),
-                math.sqrt(clusters / total),
-            ),
-            out_shape=(
-                jax.ShapeDtypeStruct((all_t, all_q), F32),
-                jax.ShapeDtypeStruct((q_rows, clusters), F32),
-            ),
-            in_specs=[vmem] * 4,
-            out_specs=(vmem, vmem),
-            scratch_shapes=[
                 pltpu.VMEM((groups, T_ALL, 128), BF16),
                 pltpu.VMEM((ne, Q_ALL, 128), BF16),
                 pltpu.VMEM((128, 128), F32),
@@ -620,6 +600,11 @@
                 pltpu.VMEM((all_t, all_q), F32),
                 pltpu.VMEM((ne, q_rows, clusters), BF16),
                 pltpu.VMEM((ne, q_rows, clusters), BF16),
+                dma((4, groups)),
+                dma((2, nz)),
+                dma((2, nz)),
+                dma((2, far, 2, 2)),
+                dma((2, far, 2, 2)),
                 dma((3, max(ne, np_))),
                 dma((3, max(ne, np_))),
                 dma((2, 2, 8)),
@@ -632,10 +617,10 @@
                 dma((ne,)),
             ],
             compiler_params=pltpu.CompilerParams(
-                collective_id=1, has_side_effects=True, vmem_limit_bytes=limit
+                collective_id=0, has_side_effects=True, vmem_limit_bytes=limit
             ),
             name="score",
-        )(fac, query_clusters, train_clusters.reshape(1, -1), pair_mask)
+        )(*flat, win, wout.T, query_clusters, train_clusters.reshape(1, -1), pair_mask)
         return (
             scores.T.reshape(1, all_q, groups, t_rows),
             sums.reshape(1, q_rows, clusters),

time: 112 us -> 102 us (0.911)
  Pallas kernels: 106 us -> 95.6 us
    pallas_call x2 -> x1, Pallas kernels: 106 us -> 95.6 us  [step(): pl.pallas_call(functools.partial(kernel, nz, ne, float(total * tokens), 1...]
where the time goes in v3:
time: 102 us; the launch traced here: 101 us
  Pallas kernels  95.6 us (94%)
  local copies, waits for them, and re-layouts  4.53 us (4%)
    pallas_call x1, Pallas kernels, step(): pl.pallas_call(functools.partial(kernel, nz, ne, float(total * tokens), 1...  95.6 us
    unnamed x2, local copies, waits for them, and re-layouts  3.18 us

profile of v3, /device:TPU:2, one launch (start us, length us, event | category | flops | bytes accessed | tf_op | source)
XLA Modules:
  0.0 100.8 jit_solution(2297757087149586017)
XLA Ops:
  0.6 1.4 %reshape.29.train_ids = s32[1,512]{1,0:T(1,128)} reshape(s32[16,32]{1,0:T(8,128)} %param.16) | data formatting | bytes 4096 | tf_op jit(solution)/shard_map/reshape | solution.py:623
  2.0 95.6 %score.1 = (f32[512,256]{1,0:T(8,128)}, f32[16,128]{1,0:T(8,128)}) custom-call(bf16[16,256,256]{2,1,0:T(8,128)(2,1)} %bitcast.11, bf16[16,256,256]{2,1,0:T(8,128)(2,1)} %bitcast.12, bf16[16,512,256]{2,1,0:T(8,128)(2,1)} %bitcast.9, bf16[16,512,256]{2,1,0:T(8,128)(2,1)} %bitcast.10, bf16[256,128]{1,0:T(8,128)(2,1)} %win.1, bf16[64,256]{1,0:T(8,128)(2,1)} %bitcast.14, ...), custom_call_target="tpu_custom_call" | custom-call | tf_op jit(solution)/shard_map/score/pallas_call | solution.py:560
  97.6 1.9 %copy.13 = f32[1,256,16,32]{1,3,2,0:T(8,128)} copy(f32[1,256,16,32]{1,3,2,0:T(8,128)} %bitcast.13) | data formatting | bytes 1048576
  99.5 1.3 %copy.14 = f32[1,16,128]{2,1,0:T(8,128)} copy(f32[1,16,128]{2,1,0:T(8,128)} %bitcast.15) | data formatting | bytes 16384

commit v4 on v3

--- a/solution.py
+++ b/solution.py
@@ -101,21 +101,24 @@
         core = jnp.where(u % 2 == 0, 1 - c, c)
         return lax.rem(z + shift(k), nz) * 2 + core
 
-    pairs = ((ta, ta_b), (tg, tg_b), (qa, qa_b), (qg, qg_b))
-
-    def loads(u):
+    pairs = (((ta, ta_b), (tg, tg_b)), ((qa, qa_b), (qg, qg_b)))
+
+    def loads(u, chunk):
         g = group(u)
         return [
-            pltpu.make_async_copy(src.at[g], dst.at[u], in_sem.at[i, u])
-            for i, (src, dst) in enumerate(pairs)
+            pltpu.make_async_copy(src.at[g], dst.at[u], in_sem.at[2 * chunk + i, u])
+            for i, (src, dst) in enumerate(pairs[chunk])
         ]
 
-    def start(u, carry):
-        for copy in loads(u):
-            copy.start()
-        return carry
-
-    lax.fori_loop(0, 2 * nz, start, 0)
+    for chunk in (0, 1):
+
+        def start(u, carry):
+            for copy in loads(u, chunk):
+                copy.start()
+            return carry
+
+        lax.fori_loop(0, 2 * nz, start, 0)
+
     barrier = pltpu.get_barrier_semaphore()
 
     def greet(o, carry):
@@ -137,8 +140,9 @@
     width = mask.shape[0]
     cluster_q = lax.broadcasted_iota(jnp.int32, (width, query_ids.shape[1]), 0)
     hot_q = jnp.where(cluster_q == query_ids[...], 1.0, 0.0)
-    cluster_t = lax.broadcasted_iota(jnp.int32, (width, train_ids.shape[1]), 0)
-    hot_t = jnp.where(cluster_t == train_ids[...], 1.0, 0.0)
+    ids = jnp.concatenate([train_ids[g : g + 1, :] for g in range(train_ids.shape[0])], axis=1)
+    cluster_t = lax.broadcasted_iota(jnp.int32, (width, ids.shape[1]), 0)
+    hot_t = jnp.where(cluster_t == ids, 1.0, 0.0)
     picked = dot(mask[...].astype(F32).T.astype(BF16), hot_q.astype(BF16))
     allow[...] = dot(hot_t.T.astype(BF16), picked.astype(BF16))
 
@@ -157,8 +161,8 @@
             parts[chunk].at[0, k], sibs[chunk].at[k], sib_send.at[chunk, k], sib_recv.at[chunk, k], sibling
         )
 
-    def project(u, carry):
-        for copy in loads(u):
+    def project_train(u):
+        for copy in loads(u, 0):
             copy.wait()
         k, own = u // 2, u % 2
         part_t[own, k, 0:T_IN, :] = dot(ta_b[u], w_in).astype(BF16)
@@ -170,14 +174,16 @@
         def _():
             to_sibling(k, 0).start()
 
+    def project_query(u):
+        for copy in loads(u, 1):
+            copy.wait()
+        k, own = u // 2, u % 2
         part_q[own, k, 0:Q_IN, :] = dot(qa_b[u], w_in)
         part_q[own, k, Q_IN:Q_ALL, :] = dot(qg_b[u, 0:128, :], w_low) + dot(qg_b[u, 128:256, :], w_high)
 
         @pl.when(own == 0)
         def _():
             to_sibling(k, 1).start()
-
-        return carry
 
     def hop(way, step, chunk, half):
         rows = halves(chunk)[half]
@@ -370,20 +376,25 @@
 
         loop(low, high, one)
 
+    def sibling_sent(low, high, chunk):
+        for k in range(low, high):
+            to_sibling(k, chunk).wait_recv()
+
     for step in range(far):
-        low, high = (0, 2) if step == 0 else (4 * step - 2, 4 * step + 2)
-        lax.fori_loop(low, high, project, 0)
-        for k in range(low // 2, high // 2):
-            to_sibling(k, 0).wait_recv()
-            to_sibling(k, 1).wait_recv()
+        low, high = (0, 1) if step == 0 else (2 * step - 1, 2 * step + 1)
+        loop(2 * low, 2 * high, project_train)
+        sibling_sent(low, high, 0)
         if step:
             short(step, 0)
         long(step, 0)
+    loop(0, 6, project_query)
+    sibling_sent(0, 1, 1)
     long(0, 1)
+    loop(2 * nz - 2, 2 * nz, project_train)
+    sibling_sent(1, 3, 1)
     short(1, 1)
-    lax.fori_loop(2 * nz - 2, 2 * nz, project, 0)
-    to_sibling(nz - 1, 0).wait_recv()
-    to_sibling(nz - 1, 1).wait_recv()
+    loop(6, 2 * nz, project_query)
+    sibling_sent(nz - 1, nz, 0)
 
     def put_train(rows, value):
         tf[p, rows, :] = value
@@ -411,6 +422,7 @@
     s1[...] = total(g1, ne)
     loop(1, np_, lambda o: column(o).start())
     g2[p] = s1[...]
+    sibling_sent(3, nz, 1)
     short(2, 1)
     long(2, 1)
     for way in (0, 1):
@@ -438,23 +450,6 @@
         [jnp.concatenate([inv_out, zero], axis=1), jnp.concatenate([zero, inv_out], axis=1)], axis=0
     )
 
-    final(1, put_query)
-    q_start(0, 2)
-    form_trains(2, 6)
-    q_wait(0)
-    q_start(1, 3, 4)
-    relay(2)
-    q_wait(1)
-    q_start(5)
-    form_trains(6, 10)
-    for o, way in both_ways:
-        for index in (0, 1):
-            q_copy(o, way, 2 + 2 * way + index, False).wait_recv()
-            q_copy(o, way, 6 + index, True).start()
-    for step in range(3, far + 1):
-        relay(step)
-    form_trains(10, 2 * nz)
-
     def thirds(x):
         high = x.astype(BF16)
         mid, low = split(x - high.astype(F32))
@@ -480,12 +475,49 @@
 
         put(qmat, pl.multiple_of(i * 16, 16), product(0), product(1))
 
+    final(1, put_query)
+    q_start(0, 2)
+    form_trains(2, 6)
+    q_wait(0)
+    q_start(1, 3, 4)
+    q_wait(1)
+    q_start(5)
+    form_query(e)
+    relay(2)
+    q_wait(2)
+
+    def near(i):
+        step = 2 * (i % 2) - 1
+        form_query(place(0, jnp.where(i < 2, step, 0), jnp.where(i < 2, 0, step)))
+
+    loop(0, 4, near)
+    q_wait(3, 4)
     for o, way in both_ways:
-        for slot in (4 - 2 * way, 5 - 2 * way, 6, 7):
-            q_copy(o, way, slot, False).wait_recv()
-    loop(0, ne, form_query)
-
-    deep = 1024
+        for index in (0, 1):
+            if way and index:
+                q_copy(o, way, 5, False).wait_recv()
+            q_copy(o, way, 6 + index, True).start()
+
+    def corner(i):
+        form_query(place(0, 2 * (i % 2) - 1, 2 * (i // 2) - 1))
+
+    loop(0, 4, corner)
+    for step in range(3, far):
+        relay(step)
+    form_trains(6, 10)
+    relay(far)
+    form_trains(10, 2 * nz)
+
+    for o in (0, 1):
+        q_copy(o, 0, 5, False).wait_recv()
+    q_wait(6, 7)
+
+    def distant(i):
+        form_query(place(0, jnp.where(i < 4, 2, i - 5), jnp.where(i < 4, i - 1, 2)))
+
+    loop(0, 7, distant)
+
+    deep = 2048
     raw[...] = jnp.zeros_like(raw)
 
     def contract(i):
@@ -620,7 +652,7 @@
                 collective_id=0, has_side_effects=True, vmem_limit_bytes=limit
             ),
             name="score",
-        )(*flat, win, wout.T, query_clusters, train_clusters.reshape(1, -1), pair_mask)
+        )(*flat, win, wout.T, query_clusters, train_clusters, pair_mask)
         return (
             scores.T.reshape(1, all_q, groups, t_rows),
             sums.reshape(1, q_rows, clusters),

time: 102 us -> 95.7 us (0.938)
  Pallas kernels: 95.6 us -> 91.2 us
  local copies, waits for them, and re-layouts: 4.53 us -> 3.18 us
    pallas_call x1, Pallas kernels: 95.6 us -> 91.2 us  [step(): pl.pallas_call(functools.partial(kernel, nz, ne, float(total * tokens), 1...]
    reshape x1 -> x0, local copies, waits for them, and re-layouts: 1.35 us -> none  [step(): train_clusters.reshape(1, -1)]
where the time goes in v4:
time: 95.7 us; the launch traced here: 95.1 us
  Pallas kernels  91.2 us (95%)
  local copies, waits for them, and re-layouts  3.18 us (3%)
    pallas_call x1, Pallas kernels, step(): pl.pallas_call(functools.partial(kernel, nz, ne, float(total * tokens), 1...  91.2 us
    unnamed x2, local copies, waits for them, and re-layouts  3.18 us

profile of v4, /device:TPU:2, one launch (start us, length us, event | category | flops | bytes accessed | tf_op | source)
XLA Modules:
  0.0 95.1 jit_solution(10595535163228338881)
XLA Ops:
  0.6 91.2 %score.1 = (f32[512,256]{1,0:T(8,128)}, f32[16,128]{1,0:T(8,128)}) custom-call(bf16[16,256,256]{2,1,0:T(8,128)(2,1)} %bitcast.11, bf16[16,256,256]{2,1,0:T(8,128)(2,1)} %bitcast.12, bf16[16,512,256]{2,1,0:T(8,128)(2,1)} %bitcast.9, bf16[16,512,256]{2,1,0:T(8,128)(2,1)} %bitcast.10, bf16[256,128]{1,0:T(8,128)(2,1)} %win.1, bf16[64,256]{1,0:T(8,128)(2,1)} %bitcast.14, ...), custom_call_target="tpu_custom_call" | custom-call | tf_op jit(solution)/shard_map/score/pallas_call | solution.py:592
  91.9 1.9 %copy.13 = f32[1,256,16,32]{1,3,2,0:T(8,128)} copy(f32[1,256,16,32]{1,3,2,0:T(8,128)} %bitcast.13) | data formatting | bytes 1048576
  93.8 1.3 %copy.14 = f32[1,16,128]{2,1,0:T(8,128)} copy(f32[1,16,128]{2,1,0:T(8,128)} %bitcast.15) | data formatting | bytes 16384
